TPU v7x, 32 devices: a whole 2x2x4 slice. The times are simulated.
32 devices in a mesh: strip: 4 (over z), mr: 8 (over y, x, core).
Axes of the slice: x: 2, y: 2, z: 4, core: 2. Of those that a mesh axis runs over, the one named last changes fastest.
Arguments:
- alm: bfloat16 [2, 256, 2048], P(None, ('strip', 'mr')), may hold values from -6 to 6
- beam: float32 [13, 2048], replicated, may hold values from -6 to 6
- wigner: bfloat16 [256, 13, 32, 2048], P(('strip', 'mr')), may hold values from -0.125 to 0.125
- base_index: int32 [8192], P(('strip', 'mr')), may hold values from 0 to 16124
- interp_weights: float32 [12, 8192], P(None, ('strip', 'mr')), may hold values from -3 to 3
- live_counts: int32 [32, 32], P(('strip', 'mr')), may hold values from 0 to 8, as said below
Outputs:
- tod: float32 [8192], P(('strip', 'mr'))
Inputs may be any that keep to these rules, and one draw needn't show every extreme that they name: live_counts[i, d] counts the used slots from device i to block d; blocks differ in how many samples point into them, and some pair uses all 8 slots in every draw.
All inputs are finite; a program needn't handle non-finite values.
Results may differ from a plain program's by a relative error of at most 0.0055.
Values may be sent and summed in bfloat16 or wider, within the bound.
No kernel may reach another device: no remote copies, remote signals or barrier semaphores. Data moves between devices by JAX's collectives and lax.ppermute only.
A program may use at most 64 MiB of HBM per device.

v0:
```python
import math
import jax
import jax.numpy as jnp
from jax import lax
from jax.sharding import PartitionSpec as P


def padded_2(x, sides, width):
    for axis, dim in sides:
        devices, length = (lax.axis_size(axis), x.shape[dim])
        up = [(i, (i + 1) % devices) for i in range(devices)]
        down = [(j, i) for i, j in up]
        last = lax.slice_in_dim(x, length - width, length, axis=dim)
        first = lax.slice_in_dim(x, 0, width, axis=dim)
        before = lax.ppermute(last, axis, up)
        after = lax.ppermute(first, axis, down)
        x = jnp.concatenate([before, x, after], axis=dim)
    return x


def phase_tables(m_first, m_count, phi_count, phi_total):
    m_vals = m_first + jnp.arange(m_count, dtype=jnp.int32)
    phi_vals = jnp.arange(phi_count, dtype=jnp.int32)
    product = phi_vals[:, None] * m_vals[None, :] % phi_total
    angle = 2.0 * math.pi / phi_total * product.astype(jnp.float32)
    return (jnp.cos(angle).astype(jnp.bfloat16), jnp.sin(angle).astype(jnp.bfloat16))


def orient_table(psi_count, k_count):
    product = (
        jnp.arange(psi_count, dtype=jnp.int32)[:, None]
        * jnp.arange(k_count, dtype=jnp.int32)[None, :]
        % psi_count
    )
    angle = 2.0 * math.pi / psi_count * product.astype(jnp.float32)
    return jnp.stack([jnp.cos(angle), -jnp.sin(angle)], axis=1)


def phi_sum(cos_table, sin_table, coef):
    real_part = jnp.dot(cos_table, coef[0], preferred_element_type=jnp.float32) - jnp.dot(
        sin_table, coef[1], preferred_element_type=jnp.float32
    )
    imag_part = jnp.dot(sin_table, coef[0], preferred_element_type=jnp.float32) + jnp.dot(
        cos_table, coef[1], preferred_element_type=jnp.float32
    )
    return jnp.concatenate([real_part, imag_part], axis=1)


def decode(base, lat_dev, phi_dev):
    phi_base = base % (phi_dev + 1)
    rest = base // (phi_dev + 1)
    return (rest // (lat_dev + 1), rest % (lat_dev + 1), phi_base)


def tap_table(index, tap_weights, length):
    positions = jnp.arange(length, dtype=jnp.int32)[:, None]
    table = jnp.zeros((length, index.shape[1]), jnp.float32)
    for offset in range(4):
        table = table + jnp.where(
            positions == index[offset][None, :], tap_weights[offset][None, :], 0.0
        )
    return table


def stencil(cube_block, psi_idx, lat_idx, phi_idx, weights, lat_weight):
    psi_len, lat_len, phi_len = cube_block.shape
    phi_table = tap_table(phi_idx, weights[4:8], phi_len)
    lat_table = tap_table(lat_idx, lat_weight, lat_len)
    psi_table = tap_table(psi_idx, weights[8:12], psi_len)
    along = jnp.dot(
        cube_block.reshape(psi_len * lat_len, phi_len).astype(jnp.float32),
        phi_table,
        precision=lax.Precision.HIGHEST,
    )
    along = along.reshape(psi_len, lat_len, -1)
    across = jnp.sum(along * lat_table[None], axis=1)
    return jnp.sum(across * psi_table, axis=0)


def owner_values(packet_in, padded, lat_dev, phi_dev, psi_count):
    shape = packet_in.shape[1:]
    flat = packet_in.reshape(packet_in.shape[0], -1)
    psi_base, lat_base, phi_base = decode(flat[12].astype(jnp.int32), lat_dev, phi_dev)
    offs = jnp.arange(4, dtype=jnp.int32)[:, None]
    psi_idx = (psi_base[None] + offs) % psi_count
    lat_idx = lat_base[None] + offs
    phi_idx = phi_base[None] + offs
    return stencil(padded, psi_idx, lat_idx, phi_idx, flat[:12], flat[0:4]).reshape(shape)


def on_device(alm, beam, wigner, base_index, interp_weights, live_counts):
    n_strip = lax.axis_size("strip")
    n_mr = lax.axis_size("mr")
    devices = n_strip * n_mr
    k_count = beam.shape[0]
    mixed = (alm[:, :, None, :].astype(jnp.float32) * beam[None, None, :, :]).astype(jnp.bfloat16)
    coef = jnp.einsum("cmkl,mkrl->cmkr", mixed, wigner, preferred_element_type=jnp.float32).astype(
        jnp.bfloat16
    )
    coef = lax.all_to_all(coef, "mr", split_axis=3, concat_axis=1, tiled=True)
    m_here = coef.shape[1]
    lat_dev = coef.shape[3]
    coef = coef.reshape(2, m_here, k_count * lat_dev)
    m_total = m_here * n_strip
    phi_total = 2 * m_total
    phi_dev = phi_total // n_strip
    strip_at = lax.axis_index("strip")
    m_first = strip_at * m_here
    cos_table, sin_table = phase_tables(
        m_first, m_here, phi_dev * lax.axis_size("strip"), phi_total
    )
    spectra = lax.psum_scatter(
        phi_sum(cos_table, sin_table, coef), "strip", scatter_dimension=0, tiled=True
    )
    spectra = spectra.reshape(phi_dev, 2, k_count, lat_dev)
    psi_count = 2 * k_count - 1
    scale = 1.0 / math.sqrt(m_total * k_count)
    cube = (
        jnp.einsum(
            "pckr,tck->trp",
            spectra,
            orient_table(psi_count, k_count),
            precision=lax.Precision.HIGHEST,
        )
        * scale
    ).astype(jnp.bfloat16)
    cap = base_index.shape[0] // devices
    live = (
        jnp.arange(cap, dtype=jnp.int32)[None, :] < live_counts.reshape(devices)[:, None]
    ).astype(jnp.float32)
    weights = interp_weights.reshape(12, devices, cap)
    lat_w = weights[0:4] * live[None]
    weights = jnp.concatenate([lat_w, weights[4:]], axis=0)
    padded = padded_2(cube, (("strip", 2), ("mr", 1)), 2)
    packet = jnp.concatenate(
        [weights, base_index.reshape(1, devices, cap).astype(jnp.float32)], axis=0
    )
    values = owner_values(
        lax.all_to_all(packet, ("strip", "mr"), split_axis=1, concat_axis=1, tiled=True),
        padded,
        lat_dev,
        phi_dev,
        psi_count,
    )
    result = lax.all_to_all(values, ("strip", "mr"), split_axis=0, concat_axis=0, tiled=True)
    return result.reshape(-1)


def solution(mesh):
    placed = (
        P(None, ("strip", "mr"), None),
        P(),
        P(("strip", "mr"), None, None, None),
        P(("strip", "mr")),
        P(None, ("strip", "mr")),
        P(("strip", "mr"), None),
    )
    return jax.shard_map(
        on_device, mesh=mesh, in_specs=placed, out_specs=P(("strip", "mr")), check_vma=False
    )
```

profile of v0, /device:TPU:0, one launch (start us, length us, event | category | flops | bytes accessed | tf_op | source)
XLA Modules:
  0.0 91.3 jit_solution(9475546606668094492)
XLA Ops:
  6.5 1.0 %copy.40 = f32[2,8,2048]{2,0,1:T(2,128)S(1)} copy(bf16[2,8,2048]{2,1,0:T(8,128)(2,1)} %param.6) | data formatting | bytes 196608 | tf_op jit(solution)/shard_map/convert_element_type | solution.py:96
  7.5 6.8 %fusion.2 = bf16[2,8,13,32]{3,0,2,1:T(2,128)(2,1)S(1)} fusion(bf16[8,13,32,2048]{3,2,1,0:T(8,128)(2,1)} %param.8, f32[13,2048]{1,0:T(8,128)} %param.7, f32[2,8,2048]{2,0,1:T(2,128)S(1)} %copy.40), kind=kOutput, calls=%fused_computation.8 | convolution fusion | flops 28121600 | bytes 13882368 | tf_op jit(solution)/shard_map/cmkl,mkrl->cmkr/dot_general | solution.py:97
  14.4 0.2 copy.41
  14.6 0.8 reshape.386
  15.4 5.2 %all-to-all-start = ((bf16[8,2,416]{2,1,0:T(2,128)(2,1)}), bf16[8,2,416]{2,1,0:T(2,128)(2,1)S(1)}, u32[]{:S(2)}, u32[]{:S(2)}) async-start(bf16[8,2,416]{2,1,0:T(2,128)(2,1)} %reshape.386), calls=%async_computation | async-start | bytes 32768 | tf_op jit(solution)/shard_map/all_to_all | solution.py:100
  21.1 0.9 %copy.46 = f32[13,32,8]{0,2,1:T(8,128)} copy(f32[13,32,8]{2,1,0:T(8,128)S(1)} %pad_maximum_fusion.1) | data formatting | bytes 26624 | tf_op jit(solution)/shard_map/concatenate | solution.py:135
  22.0 3.3 %all-to-all-done = bf16[8,2,416]{2,1,0:T(2,128)(2,1)S(1)} async-done(((bf16[8,2,416]{2,1,0:T(2,128)(2,1)}), bf16[8,2,416]{2,1,0:T(2,128)(2,1)S(1)}, u32[]{:S(2)}, u32[]{:S(2)}) %all-to-all-start) | async-done | bytes 13344 | tf_op jit(solution)/shard_map/all_to_all | solution.py:100
  25.3 4.0 %all-to-all-start.1 = ((f32[13,32,8]{0,2,1:T(8,128)}), f32[13,32,8]{0,2,1:T(8,128)S(1)}, u32[]{:S(2)}, u32[]{:S(2)}) async-start(f32[13,32,8]{0,2,1:T(8,128)} %copy.46), calls=%async_computation.2 | async-start | bytes 262144 | tf_op jit(solution)/shard_map/all_to_all | solution.py:139
  29.3 0.3 reshape.387
  29.7 0.3 copy.43
  30.0 0.1 squeeze.4
  30.1 1.3 %fusion.22 = f32[512,52]{0,1:T(8,128)S(1)} fusion(bf16[64,52]{0,1:T(8,128)(2,1)S(1)} %squeeze.4, s32[64]{0:T(128)S(1)} %iota_add_fusion.2), kind=kOutput, calls=%fused_computation.55 | convolution fusion | flops 3899392 | bytes 113408 | tf_op jit(solution)/shard_map/dot_general | solution.py:43
  31.4 1.3 %fusion.21 = f32[512,52]{0,1:T(8,128)S(1)} fusion(bf16[64,52]{0,1:T(8,128)(2,1)S(1)} %squeeze.4, s32[64]{0:T(128)S(1)} %iota_add_fusion.2), kind=kOutput, calls=%fused_computation.54 | convolution fusion | flops 3899392 | bytes 113408 | tf_op jit(solution)/shard_map/dot_general | solution.py:40
  32.7 0.3 copy.44
  33.1 1.3 %convolution_add_fusion = f32[512,52]{0,1:T(8,128)S(1)} fusion(f32[512,52]{0,1:T(8,128)S(1)} %fusion.22, bf16[64,52]{0,1:T(8,128)(2,1)S(1)} %squeeze.10, s32[64]{0:T(128)S(1)} %iota_add_fusion.2), kind=kOutput, calls=%fused_computation.3 | convolution fusion | flops 3926016 | bytes 219904 | tf_op jit(solution)/shard_map/dot_general | solution.py:43
  34.4 1.3 %convolution_subtract_fusion = f32[512,52]{0,1:T(8,128)S(1)} fusion(f32[512,52]{0,1:T(8,128)S(1)} %fusion.21, bf16[64,52]{0,1:T(8,128)(2,1)S(1)} %squeeze.10, s32[64]{0:T(128)S(1)} %iota_add_fusion.2), kind=kOutput, calls=%fused_computation.4 | convolution fusion | flops 3926016 | bytes 219904 | tf_op jit(solution)/shard_map/dot_general | solution.py:40
  35.8 0.7 pad_maximum_fusion
  36.5 1.0 %all-to-all-done.1 = f32[13,32,8]{0,2,1:T(8,128)S(1)} async-done(((f32[13,32,8]{0,2,1:T(8,128)}), f32[13,32,8]{0,2,1:T(8,128)S(1)}, u32[]{:S(2)}, u32[]{:S(2)}) %all-to-all-start.1) | async-done | bytes 13344 | tf_op jit(solution)/shard_map/all_to_all | solution.py:139
  37.5 0.7 fusion.23
  38.3 1.2 %remainder_reduce_fusion = (s32[32,8]{1,0:T(8,128)S(1)}, s32[32,8]{1,0:T(8,128)S(1)}) fusion(f32[13,32,8]{0,2,1:T(8,128)S(1)} %all-to-all-done.1), kind=kLoop, calls=%fused_computation.53 | loop fusion | flops 768 | bytes 3072 | tf_op jit(solution)/shard_map/jit(remainder)/rem | solution.py:50
  39.8 0.9 slice_reduce_fusion.3
  41.1 16.3 %reduce-scatter.2.cloned.1.call-done = f32[128,104]{0,1:T(8,128)} async-done(((f32[512,104]{0,1:T(8,128)}), f32[128,104]{0,1:T(8,128)}) %reduce-scatter.2.cloned.1.call-update) | async-done | bytes 53264 | tf_op jit(solution)/shard_map/reduce_scatter | solution.py:112
  57.4 1.1 %fusion.4 = bf16[25,4,128]{2,0,1:T(8,128)(2,1)S(1)} fusion(f32[128,2,13,4]{0,3,2,1:T(4,128)} %bitcast.55, f32[25,1,13]{0,2,1:T(8,128)S(1)} %get-tuple-element.40, f32[25,1,13]{0,2,1:T(8,128)S(1)} %get-tuple-element.41), kind=kOutput, calls=%fused_computation.10 | convolution fusion | flops 4019850 | bytes 81448 | tf_op jit(solution)/shard_map/pckr,tck->trp/dot_general | solution.py:119
  58.5 3.8 %collective-permute-start.1 = (bf16[25,4,2]{2,0,1:T(8,128)(2,1)S(1)}, bf16[25,4,2]{2,0,1:T(8,128)(2,1)S(1)}, u32[]{:S(2)}, u32[]{:S(2)}) collective-permute-start(bf16[25,4,2]{2,0,1:T(8,128)(2,1)S(1)} %get-tuple-element.24), channel_id=1, source_target_pairs={{8,0},{16,8},{24,16},{0,24},{9,1},{17,9},{25,17},{1,25},{10,2},{18... | collective-permute-start | bytes 1208 | tf_op jit(solution)/shard_map/ppermute | solution.py:16
  62.4 1.9 %collective-permute-done = bf16[25,4,2]{2,0,1:T(8,128)(2,1)S(1)} collective-permute-done((bf16[25,4,2]{2,0,1:T(8,128)(2,1)S(1)}, bf16[25,4,2]{2,0,1:T(8,128)(2,1)S(1)}, u32[]{:S(2)}, u32[]{:S(2)}) %collective-permute-start) | collective-permute-done | bytes 432 | tf_op jit(solution)/shard_map/ppermute | solution.py:15
  64.4 2.6 %collective-permute-start.3 = (bf16[25,2,132]{2,0,1:T(8,128)(2,1)S(1)}, bf16[25,2,132]{2,0,1:T(8,128)(2,1)S(1)}, u32[]{:S(2)}, u32[]{:S(2)}) collective-permute-start(bf16[25,2,132]{2,0,1:T(8,128)(2,1)S(1)} %get-tuple-element.22), channel_id=1, source_target_pairs={{1,0},{2,1},{3,2},{4,3},{5,4},{6,5},{7,6},{0,7},{9,8},{10,9},{11,1... | collective-permute-start | bytes 39608 | tf_op jit(solution)/shard_map/ppermute | solution.py:16
  67.8 0.9 collective-permute-done.2
  68.8 0.4 fusion
  69.3 13.3 %all_to_all.29 = f32[32,1,8]{2,1,0:T(1,128)S(1)} all-to-all(f32[32,1,8]{2,1,0:T(1,128)S(1)} %bitcast.56), channel_id=1, replica_groups=mesh['strip'=4,'mr'=8] {'strip','mr'}, dimensions={0} | all-to-all | bytes 2048 | tf_op jit(solution)/shard_map/all_to_all | solution.py:145
  82.6 0.5 broadcast.328
  83.1 0.7 reduce.33
  83.8 0.7 reshape.358
  (55 shorter events, 2.5 us)
Async XLA Ops:
  6.5 14.0 %copy-start = (f32[12,256]{1,0:T(8,128)S(1)}, f32[12,256]{1,0:T(8,128)}, u32[]{:S(2)}) copy-start(f32[12,256]{1,0:T(8,128)} %param.10) | copy-start | bytes 36868
  6.5 14.3 %slice-start = ((f32[12,256]{1,0:T(8,128)}), f32[4,256]{1,0:T(4,128)S(1)}, s32[]{:S(2)}) async-start(f32[12,256]{1,0:T(8,128)} %param.10), calls=%async_computation.5 | async-start | bytes 8192 | tf_op jit(solution)/shard_map/slice | solution.py:132
  6.5 14.1 %copy-start.1 = (s32[256]{0:T(256)S(1)}, s32[256]{0:T(256)}, u32[]{:S(2)}) copy-start(s32[256]{0:T(256)} %param.9) | copy-start | bytes 3076
  6.5 14.2 %copy-start.2 = (s32[1,32]{1,0:T(1,128)S(1)}, s32[1,32]{1,0:T(1,128)}, u32[]{:S(2)}) copy-start(s32[1,32]{1,0:T(1,128)} %param.11) | copy-start | bytes 388
  15.4 9.9 %all-to-all-start = ((bf16[8,2,416]{2,1,0:T(2,128)(2,1)}), bf16[8,2,416]{2,1,0:T(2,128)(2,1)S(1)}, u32[]{:S(2)}, u32[]{:S(2)}) async-start(bf16[8,2,416]{2,1,0:T(2,128)(2,1)} %reshape.386), calls=%async_computation | async-start | bytes 32768 | tf_op jit(solution)/shard_map/all_to_all | solution.py:100
  25.3 12.2 %all-to-all-start.1 = ((f32[13,32,8]{0,2,1:T(8,128)}), f32[13,32,8]{0,2,1:T(8,128)S(1)}, u32[]{:S(2)}, u32[]{:S(2)}) async-start(f32[13,32,8]{0,2,1:T(8,128)} %copy.46), calls=%async_computation.2 | async-start | bytes 262144 | tf_op jit(solution)/shard_map/all_to_all | solution.py:139
  29.3 28.1 %reduce-scatter.2.cloned.1.call-start = ((), (), s32[]{:S(2)}) async-start(), calls=%async_computation.4 | async-start | bytes 266240 | tf_op jit(solution)/shard_map/reduce_scatter | solution.py:112
  58.5 5.7 %collective-permute-start = (bf16[25,4,2]{2,0,1:T(8,128)(2,1)S(1)}, bf16[25,4,2]{2,0,1:T(8,128)(2,1)S(1)}, u32[]{:S(2)}, u32[]{:S(2)}) collective-permute-start(bf16[25,4,2]{2,0,1:T(8,128)(2,1)S(1)} %get-tuple-element.23), channel_id=1, source_target_pairs={{0,8},{8,16},{16,24},{24,0},{1,9},{9,17},{17,25},{25,1},{2,10},{10... | collective-permute-start | bytes 1208 | tf_op jit(solution)/shard_map/ppermute | solution.py:15
  58.5 5.7 %collective-permute-start.1 = (bf16[25,4,2]{2,0,1:T(8,128)(2,1)S(1)}, bf16[25,4,2]{2,0,1:T(8,128)(2,1)S(1)}, u32[]{:S(2)}, u32[]{:S(2)}) collective-permute-start(bf16[25,4,2]{2,0,1:T(8,128)(2,1)S(1)} %get-tuple-element.24), channel_id=1, source_target_pairs={{8,0},{16,8},{24,16},{0,24},{9,1},{17,9},{25,17},{1,25},{10,2},{18... | collective-permute-start | bytes 1208 | tf_op jit(solution)/shard_map/ppermute | solution.py:16
  64.4 4.3 %collective-permute-start.2 = (bf16[25,2,132]{2,0,1:T(8,128)(2,1)S(1)}, bf16[25,2,132]{2,0,1:T(8,128)(2,1)S(1)}, u32[]{:S(2)}, u32[]{:S(2)}) collective-permute-start(bf16[25,2,132]{2,0,1:T(8,128)(2,1)S(1)} %get-tuple-element.21), channel_id=1, source_target_pairs={{0,1},{1,2},{2,3},{3,4},{4,5},{5,6},{6,7},{7,0},{8,9},{9,10},{10,1... | collective-permute-start | bytes 39608 | tf_op jit(solution)/shard_map/ppermute | solution.py:15
  64.4 4.2 %collective-permute-start.3 = (bf16[25,2,132]{2,0,1:T(8,128)(2,1)S(1)}, bf16[25,2,132]{2,0,1:T(8,128)(2,1)S(1)}, u32[]{:S(2)}, u32[]{:S(2)}) collective-permute-start(bf16[25,2,132]{2,0,1:T(8,128)(2,1)S(1)} %get-tuple-element.22), channel_id=1, source_target_pairs={{1,0},{2,1},{3,2},{4,3},{5,4},{6,5},{7,6},{0,7},{9,8},{10,9},{11,1... | collective-permute-start | bytes 39608 | tf_op jit(solution)/shard_map/ppermute | solution.py:16
Sparse Core Ops, SparseCore 0:
  36.6 20.7 reduce-scatter.1
where the time goes:
time: 91.6 us; the launch traced here: 91.3 us
  waiting for transfers between devices  23.4 us (26%)
  starting transfers between devices  15.7 us (17%)
  between operations  13.7 us (15%)
  matrix products  13.4 us (15%)
  blocking collectives  13.3 us (15%)
  local copies, waits for them, and re-layouts  7.98 us (9%)
  other arithmetic  3.78 us (4%)
    reduce_scatter x1, waiting for transfers between devices, on_device(): lax.psum_scatter(phi_sum(cos_table, sin_table, coef), 'strip', scatter_di...  16.3 us
    all_to_all x1, blocking collectives, on_device(): lax.all_to_all(values, ('strip', 'mr'), split_axis=0, concat_axis=0, tile...  13.3 us
    dot_general x1, matrix products, on_device(): jnp.einsum('cmkl,mkrl->cmkr', mixed, wigner, preferred_element_type=jnp.f...  6.85 us
    ppermute x2, starting transfers between devices, padded_2(): after = lax.ppermute(first, axis, down)  6.45 us
    all_to_all x1, starting transfers between devices, on_device(): coef = lax.all_to_all(coef, 'mr', split_axis=3, concat_axis=1, tiled=True)  5.17 us
    all_to_all x1, starting transfers between devices, on_device(): lax.all_to_all(packet, ('strip', 'mr'), split_axis=1, concat_axis=1, tile...  3.97 us
    all_to_all x1, waiting for transfers between devices, on_device(): coef = lax.all_to_all(coef, 'mr', split_axis=3, concat_axis=1, tiled=True)  3.3 us
    ppermute x2, waiting for transfers between devices, padded_2(): before = lax.ppermute(last, axis, up)  2.75 us
  transfers between devices with their start and end apart: 7, of which 5 were waited for; matrix products, arithmetic and copies ran while one was open for 14% of the time, Pallas kernels for 0%

commit v1 on v0

--- a/solution.py
+++ b/solution.py
@@ -3,6 +3,7 @@
 import jax.numpy as jnp
 from jax import lax
 from jax.sharding import PartitionSpec as P
+from jax.lax import all_to_all, axis_size
 
 
 def padded_2(x, sides, width):
@@ -136,7 +137,15 @@
         [weights, base_index.reshape(1, devices, cap).astype(jnp.float32)], axis=0
     )
     values = owner_values(
-        lax.all_to_all(packet, ("strip", "mr"), split_axis=1, concat_axis=1, tiled=True),
+        jnp.concatenate(
+            all_to_all(
+                jnp.stack(jnp.split(packet, axis_size(("strip", "mr")), 1), axis=0),
+                axis_name=("strip", "mr"),
+                split_axis=0,
+                concat_axis=0,
+            ),
+            1,
+        ),
         padded,
         lat_dev,
         phi_dev,

time: 91.6 us -> 111 us (1.21)
  local copies, waits for them, and re-layouts: 7.98 us -> 28.6 us
  waiting for transfers between devices: 23.4 us -> 20.1 us
  starting transfers between devices: 15.7 us -> 18 us
    unnamed x8 -> x39, local copies, waits for them, and re-layouts: 1.11 us -> 19.4 us
    all_to_all x1, waiting for transfers between devices: 3.3 us -> 0.01 us  [on_device(): coef = lax.all_to_all(coef, 'mr', split_axis=3, concat_axis=1, tiled=True)]
    split x0 -> x34, local copies, waits for them, and re-layouts: none -> 2.66 us  [on_device(): jnp.split(packet, axis_size(('strip', 'mr')), 1)]
    all_to_all x1, starting transfers between devices: 3.97 us -> 6.32 us  [on_device(): all_to_all(jnp.stack(jnp.split(packet, axis_size(('strip', 'mr')), 1), ax...]
  transfers between devices with their start and end apart: 7 -> 7, of which waited for: 5 -> 4; matrix products, arithmetic and copies ran while one was open for 14% -> 30% of each run, Pallas kernels for 0% -> 0%
where the time goes in v1:
time: 111 us
  local copies, waits for them, and re-layouts  28.6 us (26%)
  waiting for transfers between devices  20.1 us (18%)
  starting transfers between devices  18 us (16%)
  between operations  13.8 us (12%)
  matrix products  13.4 us (12%)
  blocking collectives  13.2 us (12%)
  other arithmetic  3.78 us (3%)
    unnamed x39, local copies, waits for them, and re-layouts  19.4 us
    reduce_scatter x1, waiting for transfers between devices, on_device(): lax.psum_scatter(phi_sum(cos_table, sin_table, coef), 'strip', scatter_di...  16.3 us
    all_to_all x1, blocking collectives, on_device(): lax.all_to_all(values, ('strip', 'mr'), split_axis=0, concat_axis=0, tile...  13.2 us
    dot_general x1, matrix products, on_device(): jnp.einsum('cmkl,mkrl->cmkr', mixed, wigner, preferred_element_type=jnp.f...  6.85 us
    ppermute x2, starting transfers between devices, padded_2(): after = lax.ppermute(first, axis, down)  6.45 us
    all_to_all x1, starting transfers between devices, on_device(): all_to_all(jnp.stack(jnp.split(packet, axis_size(('strip', 'mr')), 1), ax...  6.32 us
    all_to_all x1, starting transfers between devices, on_device(): coef = lax.all_to_all(coef, 'mr', split_axis=3, concat_axis=1, tiled=True)  5.17 us
    ppermute x2, waiting for transfers between devices, padded_2(): before = lax.ppermute(last, axis, up)  2.75 us
  transfers between devices with their start and end apart: 7, of which 4 were waited for; matrix products, arithmetic and copies ran while one was open for 30% of the time, Pallas kernels for 0%

profile of v1, /device:TPU:0, one launch (start us, length us, event | category | flops | bytes accessed | tf_op | source)
XLA Modules:
  0.0 111.0 jit_solution(15138845396851755852)
XLA Ops:
  6.5 1.0 copy.351
  7.5 6.8 %fusion.2 = bf16[2,8,13,32]{3,0,2,1:T(2,128)(2,1)S(1)} fusion(bf16[8,13,32,2048]{3,2,1,0:T(8,128)(2,1)} %param.8, f32[13,2048]{1,0:T(8,128)} %param.7, f32[2,8,2048]{2,0,1:T(2,128)S(1)} %copy.351), kind=kOutput, calls=%fused_computation.8 | convolution fusion | flops 28121600 | bytes 13882368 | tf_op jit(solution)/shard_map/cmkl,mkrl->cmkr/dot_general | solution.py:98
  14.6 0.8 reshape.389
  15.4 5.2 %all-to-all-start = ((bf16[8,2,416]{2,1,0:T(2,128)(2,1)}), bf16[8,2,416]{2,1,0:T(2,128)(2,1)S(1)}, u32[]{:S(2)}, u32[]{:S(2)}) async-start(bf16[8,2,416]{2,1,0:T(2,128)(2,1)} %reshape.389), calls=%async_computation | async-start | bytes 32768 | tf_op jit(solution)/shard_map/all_to_all | solution.py:101
  24.3 0.6 constant_dynamic-update-slice_fusion.30
  26.7 0.6 constant_dynamic-update-slice_fusion.26
  29.7 0.6 constant_dynamic-update-slice_fusion.21
  33.2 0.6 constant_dynamic-update-slice_fusion.15
  35.6 0.6 constant_dynamic-update-slice_fusion.11
  39.1 0.6 constant_dynamic-update-slice_fusion.5
  39.7 0.6 constant_dynamic-update-slice_fusion.4
  41.5 0.6 constant_dynamic-update-slice_fusion.1
  42.1 0.6 constant_dynamic-update-slice_fusion
  42.7 6.3 %all-to-all-start.1 = ((f32[32,13,1,8]{1,3,2,0:T(8,128)}), f32[32,13,1,8]{1,3,2,0:T(8,128)S(1)}, u32[]{:S(2)}, u32[]{:S(2)}) async-start(f32[32,13,1,8]{1,3,2,0:T(8,128)} %constant_dynamic-update-slice_fusion), calls=%async_computation.2 | async-start | bytes 262144 | tf_op jit(solution)/shard_map/all_to_all | solution.py:141
  49.9 1.3 %fusion.22 = f32[512,52]{0,1:T(8,128)S(1)} fusion(bf16[64,52]{0,1:T(8,128)(2,1)S(1)} %squeeze.4, s32[64]{0:T(128)S(1)} %iota_add_fusion.2), kind=kOutput, calls=%fused_computation.55 | convolution fusion | flops 3899392 | bytes 113408 | tf_op jit(solution)/shard_map/dot_general | solution.py:44
  51.2 1.3 %fusion.21 = f32[512,52]{0,1:T(8,128)S(1)} fusion(bf16[64,52]{0,1:T(8,128)(2,1)S(1)} %squeeze.4, s32[64]{0:T(128)S(1)} %iota_add_fusion.2), kind=kOutput, calls=%fused_computation.54 | convolution fusion | flops 3899392 | bytes 113408 | tf_op jit(solution)/shard_map/dot_general | solution.py:41
  52.9 1.3 %convolution_add_fusion = f32[512,52]{0,1:T(8,128)S(1)} fusion(f32[512,52]{0,1:T(8,128)S(1)} %fusion.22, bf16[64,52]{0,1:T(8,128)(2,1)S(1)} %squeeze.10, s32[64]{0:T(128)S(1)} %iota_add_fusion.2), kind=kOutput, calls=%fused_computation.3 | convolution fusion | flops 3926016 | bytes 219904 | tf_op jit(solution)/shard_map/dot_general | solution.py:44
  54.2 1.3 %convolution_subtract_fusion = f32[512,52]{0,1:T(8,128)S(1)} fusion(f32[512,52]{0,1:T(8,128)S(1)} %fusion.21, bf16[64,52]{0,1:T(8,128)(2,1)S(1)} %squeeze.10, s32[64]{0:T(128)S(1)} %iota_add_fusion.2), kind=kOutput, calls=%fused_computation.4 | convolution fusion | flops 3926016 | bytes 219904 | tf_op jit(solution)/shard_map/dot_general | solution.py:41
  55.5 0.7 pad_maximum_fusion
  56.2 1.0 all-to-all-done.1
  57.2 0.7 fusion.23
  57.9 1.2 %remainder_reduce_fusion = (s32[32,8]{1,0:T(8,128)S(1)}, s32[32,8]{1,0:T(8,128)S(1)}) fusion(f32[13,32,1,8]{0,3,2,1:T(8,128)S(1)} %bitcast.118), kind=kLoop, calls=%fused_computation.53 | loop fusion | flops 768 | bytes 3072 | tf_op jit(solution)/shard_map/jit(remainder)/rem | solution.py:51
  59.2 0.9 slice_reduce_fusion.3
  60.8 16.3 %reduce-scatter.2.cloned.1.call-done = f32[128,104]{0,1:T(8,128)} async-done(((f32[512,104]{0,1:T(8,128)}), f32[128,104]{0,1:T(8,128)}) %reduce-scatter.2.cloned.1.call-update) | async-done | bytes 53264 | tf_op jit(solution)/shard_map/reduce_scatter | solution.py:113
  77.1 1.1 fusion.4
  78.3 3.8 %collective-permute-start.1 = (bf16[25,4,2]{2,0,1:T(8,128)(2,1)S(1)}, bf16[25,4,2]{2,0,1:T(8,128)(2,1)S(1)}, u32[]{:S(2)}, u32[]{:S(2)}) collective-permute-start(bf16[25,4,2]{2,0,1:T(8,128)(2,1)S(1)} %get-tuple-element.56), channel_id=1, source_target_pairs={{8,0},{16,8},{24,16},{0,24},{9,1},{17,9},{25,17},{1,25},{10,2},{18... | collective-permute-start | bytes 1208 | tf_op jit(solution)/shard_map/ppermute | solution.py:17
  82.1 1.9 %collective-permute-done = bf16[25,4,2]{2,0,1:T(8,128)(2,1)S(1)} collective-permute-done((bf16[25,4,2]{2,0,1:T(8,128)(2,1)S(1)}, bf16[25,4,2]{2,0,1:T(8,128)(2,1)S(1)}, u32[]{:S(2)}, u32[]{:S(2)}) %collective-permute-start) | collective-permute-done | bytes 432 | tf_op jit(solution)/shard_map/ppermute | solution.py:16
  84.2 2.6 %collective-permute-start.3 = (bf16[25,2,132]{2,0,1:T(8,128)(2,1)S(1)}, bf16[25,2,132]{2,0,1:T(8,128)(2,1)S(1)}, u32[]{:S(2)}, u32[]{:S(2)}) collective-permute-start(bf16[25,2,132]{2,0,1:T(8,128)(2,1)S(1)} %get-tuple-element.54), channel_id=1, source_target_pairs={{1,0},{2,1},{3,2},{4,3},{5,4},{6,5},{7,6},{0,7},{9,8},{10,9},{11,1... | collective-permute-start | bytes 39608 | tf_op jit(solution)/shard_map/ppermute | solution.py:17
  87.5 0.9 collective-permute-done.2
  89.0 13.2 %all_to_all.29 = f32[32,1,8]{2,1,0:T(1,128)S(1)} all-to-all(f32[32,1,8]{2,1,0:T(1,128)S(1)} %bitcast.124), channel_id=1, replica_groups=mesh['strip'=4,'mr'=8] {'strip','mr'}, dimensions={0} | all-to-all | bytes 2048 | tf_op jit(solution)/shard_map/all_to_all | solution.py:154
  102.8 0.7 reduce.33
  103.5 0.7 reshape.361
  (120 shorter events, 20.9 us)
Async XLA Ops:
  6.5 14.0 %copy-start = (f32[12,256]{1,0:T(8,128)S(1)}, f32[12,256]{1,0:T(8,128)}, u32[]{:S(2)}) copy-start(f32[12,256]{1,0:T(8,128)} %param.10) | copy-start | bytes 36868
  6.5 14.3 %slice-start = ((f32[12,256]{1,0:T(8,128)}), f32[4,256]{1,0:T(4,128)S(1)}, s32[]{:S(2)}) async-start(f32[12,256]{1,0:T(8,128)} %param.10), calls=%async_computation.5 | async-start | bytes 8192 | tf_op jit(solution)/shard_map/slice | solution.py:133
  6.5 14.1 %copy-start.1 = (s32[256]{0:T(256)S(1)}, s32[256]{0:T(256)}, u32[]{:S(2)}) copy-start(s32[256]{0:T(256)} %param.9) | copy-start | bytes 3076
  6.5 14.2 %copy-start.2 = (s32[1,32]{1,0:T(1,128)S(1)}, s32[1,32]{1,0:T(1,128)}, u32[]{:S(2)}) copy-start(s32[1,32]{1,0:T(1,128)} %param.11) | copy-start | bytes 388
  15.4 27.3 %all-to-all-start = ((bf16[8,2,416]{2,1,0:T(2,128)(2,1)}), bf16[8,2,416]{2,1,0:T(2,128)(2,1)S(1)}, u32[]{:S(2)}, u32[]{:S(2)}) async-start(bf16[8,2,416]{2,1,0:T(2,128)(2,1)} %reshape.389), calls=%async_computation | async-start | bytes 32768 | tf_op jit(solution)/shard_map/all_to_all | solution.py:101
  42.7 14.6 %all-to-all-start.1 = ((f32[32,13,1,8]{1,3,2,0:T(8,128)}), f32[32,13,1,8]{1,3,2,0:T(8,128)S(1)}, u32[]{:S(2)}, u32[]{:S(2)}) async-start(f32[32,13,1,8]{1,3,2,0:T(8,128)} %constant_dynamic-update-slice_fusion), calls=%async_computation.2 | async-start | bytes 262144 | tf_op jit(solution)/shard_map/all_to_all | solution.py:141
  49.0 28.1 %reduce-scatter.2.cloned.1.call-start = ((), (), s32[]{:S(2)}) async-start(), calls=%async_computation.4 | async-start | bytes 266240 | tf_op jit(solution)/shard_map/reduce_scatter | solution.py:113
  78.3 5.7 %collective-permute-start = (bf16[25,4,2]{2,0,1:T(8,128)(2,1)S(1)}, bf16[25,4,2]{2,0,1:T(8,128)(2,1)S(1)}, u32[]{:S(2)}, u32[]{:S(2)}) collective-permute-start(bf16[25,4,2]{2,0,1:T(8,128)(2,1)S(1)} %get-tuple-element.55), channel_id=1, source_target_pairs={{0,8},{8,16},{16,24},{24,0},{1,9},{9,17},{17,25},{25,1},{2,10},{10... | collective-permute-start | bytes 1208 | tf_op jit(solution)/shard_map/ppermute | solution.py:16
  78.3 5.7 %collective-permute-start.1 = (bf16[25,4,2]{2,0,1:T(8,128)(2,1)S(1)}, bf16[25,4,2]{2,0,1:T(8,128)(2,1)S(1)}, u32[]{:S(2)}, u32[]{:S(2)}) collective-permute-start(bf16[25,4,2]{2,0,1:T(8,128)(2,1)S(1)} %get-tuple-element.56), channel_id=1, source_target_pairs={{8,0},{16,8},{24,16},{0,24},{9,1},{17,9},{25,17},{1,25},{10,2},{18... | collective-permute-start | bytes 1208 | tf_op jit(solution)/shard_map/ppermute | solution.py:17
  84.1 4.3 %collective-permute-start.2 = (bf16[25,2,132]{2,0,1:T(8,128)(2,1)S(1)}, bf16[25,2,132]{2,0,1:T(8,128)(2,1)S(1)}, u32[]{:S(2)}, u32[]{:S(2)}) collective-permute-start(bf16[25,2,132]{2,0,1:T(8,128)(2,1)S(1)} %get-tuple-element.53), channel_id=1, source_target_pairs={{0,1},{1,2},{2,3},{3,4},{4,5},{5,6},{6,7},{7,0},{8,9},{9,10},{10,1... | collective-permute-start | bytes 39608 | tf_op jit(solution)/shard_map/ppermute | solution.py:16
  84.2 4.2 %collective-permute-start.3 = (bf16[25,2,132]{2,0,1:T(8,128)(2,1)S(1)}, bf16[25,2,132]{2,0,1:T(8,128)(2,1)S(1)}, u32[]{:S(2)}, u32[]{:S(2)}) collective-permute-start(bf16[25,2,132]{2,0,1:T(8,128)(2,1)S(1)} %get-tuple-element.54), channel_id=1, source_target_pairs={{1,0},{2,1},{3,2},{4,3},{5,4},{6,5},{7,6},{0,7},{9,8},{10,9},{11,1... | collective-permute-start | bytes 39608 | tf_op jit(solution)/shard_map/ppermute | solution.py:17
Sparse Core Ops, SparseCore 0:
  56.3 20.7 reduce-scatter.1
